TPU v7x, 32 devices: a whole 2x2x4 slice. The times are simulated.
32 devices in a mesh: width: 4 (over z), row: 4 (over y, core), src: 2 (over x).
Axes of the slice: x: 2, y: 2, z: 4, core: 2. Of those that a mesh axis runs over, the one named last changes fastest.
Arguments:
- query_rows: bfloat16 [1024, 8192], P('row', 'width'), may hold values from -150 to 150
- key_rows: bfloat16 [1024, 1024], P('src', 'width'), may hold values from -7 to 7
- value_rows: bfloat16 [1024, 1024], P('src'), may hold values from -6 to 6
- out_proj: bfloat16 [8192, 8192], P(('row', 'src'), 'width'), may hold values from -0.0625 to 0.0625
Outputs:
- share: float32 [1024, 1024], P('row', ('src', 'width'))
All inputs are finite; a program needn't handle non-finite values.
Results may differ from a plain program's by a relative error of at most 0.0014.
Values may be sent and summed in bfloat16 or wider, within the bound.
No kernel may reach another device: no remote copies, remote signals or barrier semaphores. Data moves between devices by JAX's collectives and lax.ppermute only.
A program may use at most 384 MiB of HBM per device.

v0:
```python
import math
import jax
import jax.numpy as jnp
from jax import lax
from jax.sharding import PartitionSpec as P

H = 64
KV = 8
HD = 128


def combined_all(shard, axis, combine):
    everything = jax.tree.map(lambda part: lax.all_gather(part, axis), shard)
    first = jax.tree.map(lambda part: part[0], everything)

    def step(k, so_far):
        return combine(so_far, jax.tree.map(lambda part: part[k], everything))

    return lax.fori_loop(1, lax.axis_size(axis), step, first)


def spread_positions(here_index, devices, piece_size):
    sender = jnp.arange(devices, dtype=jnp.int32)
    block_ids = sender * devices + (here_index - sender) % devices
    inner = jnp.arange(piece_size, dtype=jnp.int32)
    return (block_ids[:, None] * piece_size + inner[None, :]).reshape(-1)


def combine_stats(first, second):
    peak_one, mass_one = first
    peak_two, mass_two = second
    larger = jnp.maximum(peak_one, peak_two)
    return (larger, mass_one * jnp.exp(peak_one - larger) + mass_two * jnp.exp(peak_two - larger))


def body(query_rows, key_rows, value_rows, out_proj):
    row_devices = lax.axis_size("row")
    src_devices = lax.axis_size("src")
    here_row = lax.axis_index("row")
    here_src = lax.axis_index("src")
    row_count = query_rows.shape[0]
    col_count = key_rows.shape[0]
    piece_rows = row_count // row_devices
    piece_cols = col_count // src_devices
    group_size = H // KV
    stacked = jnp.roll(query_rows.reshape(row_devices, piece_rows, -1), here_row, axis=0)
    query_rows = lax.all_to_all(stacked, "row", split_axis=0, concat_axis=0, tiled=True).reshape(
        row_count, -1
    )
    key_stack = jnp.roll(key_rows.reshape(src_devices, piece_cols, -1), here_src, axis=0)
    value_stack = jnp.roll(value_rows.reshape(src_devices, piece_cols, -1), here_src, axis=0)
    key_stack, value_stack = (
        lax.all_to_all(key_stack, "src", split_axis=0, concat_axis=0, tiled=True),
        lax.all_to_all(value_stack, "src", split_axis=0, concat_axis=0, tiled=True),
    )
    key_rows = key_stack.reshape(col_count, -1)
    value_rows = value_stack.reshape(col_count, -1)
    row_pos = spread_positions(here_row, row_devices, piece_rows)
    col_pos = spread_positions(here_src, src_devices, piece_cols)
    local_heads = query_rows.shape[1] // HD
    local_kv = key_rows.shape[1] // HD
    queries = query_rows.reshape(row_count, local_kv, group_size, HD)
    key_heads = key_rows.reshape(col_count, local_kv, HD)
    scores = jnp.einsum("ikgd,jkd->kgij", queries, key_heads, preferred_element_type=jnp.float32)
    scores = scores.reshape(local_heads, row_count, col_count) / jnp.sqrt(jnp.float32(HD))
    causal = row_pos[:, None] >= col_pos[None, :]
    masked = jnp.where(causal, scores, jnp.float32(-1e30))
    row_peak = jnp.max(masked, axis=-1)
    row_mass = jnp.sum(jnp.where(causal, jnp.exp(masked - row_peak[..., None]), 0.0), axis=-1)
    row_peak, row_mass = combined_all((row_peak, row_mass), "src", combine_stats)
    weights = jnp.where(
        causal, jnp.exp(masked - row_peak[..., None]) / row_mass[..., None], 0.0
    ).astype(jnp.bfloat16)
    weights = lax.all_gather(weights, "width", axis=0, tiled=True)
    value_heads = value_rows.reshape(col_count, KV, HD)
    out_cols = out_proj.shape[1]
    proj_heads = out_proj.reshape(-1, HD, out_cols)
    portion = lax.all_gather(proj_heads, ("row", "src"), axis=0, tiled=True)
    head_count = portion.shape[0]
    head_ids = jnp.arange(head_count, dtype=jnp.int32)
    selector = (head_ids[:, None] // group_size == jnp.arange(KV, dtype=jnp.int32)[None, :]).astype(
        jnp.bfloat16
    )
    chosen = jnp.einsum(
        "hk,jkd->jhd", selector, value_heads, preferred_element_type=jnp.float32
    ).astype(jnp.bfloat16)
    images = jnp.einsum("jhd,hde->jhe", chosen, portion, preferred_element_type=jnp.float32).astype(
        jnp.bfloat16
    )
    row_block = math.gcd(row_count, 64)
    col_block = math.gcd(col_count, 32)
    col_steps = col_count // col_block
    turns = row_count // row_block * col_steps

    def tile(turn_index, running):
        row_start = turn_index // col_steps * row_block
        col_start = turn_index % col_steps * col_block
        row_slice = lax.dynamic_slice_in_dim(row_pos, row_start, row_block)
        col_slice = lax.dynamic_slice_in_dim(col_pos, col_start, col_block)

        def compute(unused):
            attend = lax.dynamic_slice(
                weights, (0, row_start, col_start), (H, row_block, col_block)
            )
            source_images = lax.dynamic_slice_in_dim(images, col_start, col_block, 0)
            contrib = jnp.einsum(
                "hij,jhe->ije", attend, source_images, preferred_element_type=jnp.float32
            )
            return jnp.sum(jnp.abs(contrib), axis=-1)

        def skipped(unused):
            return jnp.zeros((row_block, col_block), jnp.float32)

        result = lax.cond(jnp.max(row_slice) >= jnp.min(col_slice), compute, skipped, 0)
        return lax.dynamic_update_slice(running, result, (row_start, col_start))

    partial_value = lax.fori_loop(0, turns, tile, jnp.zeros((row_count, col_count), jnp.float32))
    partial_value = lax.all_to_all(
        lax.all_to_all(partial_value, "row", split_axis=0, concat_axis=0, tiled=True),
        "src",
        split_axis=1,
        concat_axis=1,
        tiled=True,
    )
    partial_value = jnp.roll(
        partial_value.reshape(row_devices, piece_rows, col_count), -here_row, axis=0
    ).reshape(row_count, col_count)
    partial_value = jnp.roll(
        partial_value.reshape(row_count, src_devices, piece_cols), -here_src, axis=1
    ).reshape(row_count, col_count)
    summed = lax.psum_scatter(partial_value, "width", scatter_dimension=1, tiled=True)
    totals = lax.psum(jnp.sum(summed, axis=1), ("width", "src"))
    position = (here_row * row_count + jnp.arange(row_count, dtype=jnp.int32) + 1).astype(
        jnp.float32
    )
    return position[:, None] * summed / totals[:, None]


def solution(mesh):
    placed = (P("row", "width"), P("src", "width"), P("src", None), P(("row", "src"), "width"))
    return jax.shard_map(
        body, mesh=mesh, in_specs=placed, out_specs=P("row", ("src", "width")), check_vma=False
    )
```

profile of v0, /device:TPU:0, one launch (start us, length us, event | category | flops | bytes accessed | tf_op | source)
XLA Modules:
  0.0 1261.2 jit_solution(17233729427972256463)
XLA Ops:
  23.1 13.2 %all-to-all-done.2 = bf16[4,64,2048]{2,1,0:T(8,128)(2,1)S(1)} async-done(((bf16[4,64,2048]{2,1,0:T(8,128)(2,1)}), bf16[4,64,2048]{2,1,0:T(8,128)(2,1)S(1)}, u32[]{:S(2)}, u32[]{:S(2)}) %all-to-all-start.2) | async-done | bytes 1048608 | tf_op jit(solution)/shard_map/all_to_all | solution.py:47
  51.9 9.3 copy.29
  73.0 11.0 all-to-all-done
  89.9 263.7 %all-gather.5.cloned.1.call-done = bf16[64,256,512]{2,1,0:T(8,128)(2,1)} async-done(((bf16[16,256,512]{2,1,0:T(8,128)(2,1)}), bf16[64,256,512]{2,1,0:T(8,128)(2,1)}) %all-gather.5.cloned.1.call-update) | async-done | bytes 16777232 | tf_op jit(solution)/shard_map/all_gather | solution.py:74
  353.6 56.4 %copy.31 = bf16[64,256,512]{0,1,2:T(8,128)(2,1)} copy(bf16[64,256,512]{2,1,0:T(8,128)(2,1)} %all-gather.5.cloned.1.call-done) | data formatting | bytes 33554432 | tf_op jit(solution)/shard_map/while | solution.py:117
  409.9 104.4 %all-gather.3.cloned.1.call-done = bf16[64,128,2048]{2,1,0:T(8,128)(2,1)} async-done(((bf16[8,128,2048]{2,1,0:T(8,128)(2,1)}), bf16[64,128,2048]{2,1,0:T(8,128)(2,1)}) %all-gather.3.cloned.1.call-update) | async-done | bytes 33554448 | tf_op jit(solution)/shard_map/all_gather | solution.py:78
  514.3 62.4 %convert_bitcast_fusion = bf16[512,64,2048]{2,0,1:T(8,128)(2,1)} fusion(bf16[64,128,2048]{2,1,0:T(8,128)(2,1)} %all-gather.3.cloned.1.call-done, bf16[512,64,128]{2,1,0:T(8,128)(2,1)} %convert_bitcast_fusion.1), kind=kOutput, calls=%fused_computation.7 | convolution fusion | flops 17246978048 | bytes 176160768 | tf_op jit(solution)/shard_map/jhd,hde->jhe/dot_general | solution.py:87
  576.7 111.2 %copy.30 = bf16[512,64,2048]{2,1,0:T(8,128)(2,1)} copy(bf16[512,64,2048]{2,0,1:T(8,128)(2,1)} %convert_bitcast_fusion) | data formatting | bytes 268435456 | tf_op jit(solution)/shard_map/while | solution.py:117
  688.0 449.8 %while.10 = (s32[]{:T(128)}, f32[256,512]{0,1:T(8,128)S(1)}, s32[256]{0:T(256)S(1)}, s32[512]{0:T(512)}, bf16[512,64,2048]{2,1,0:T(8,128)(2,1)}, /*index=5*/bf16...) while((s32[]{:T(128)}, f32[256,512]{0,1:T(8,128)S(1)}, ...), condition=%wide.region_8.9_spmd, body=%wide.region_2.8_spmd.sunk | while | flops 545257600 | bytes 8939890 | solution.py:117
  691.3 6.0 conditional.2
  770.1 6.0 conditional.2
  780.6 6.0 conditional.2
  791.1 6.0 conditional.2
  801.6 6.0 conditional.2
  812.0 6.0 conditional.2
  833.0 6.0 conditional.2
  843.5 6.0 conditional.2
  889.5 6.0 conditional.2
  899.5 6.0 conditional.2
  909.5 6.0 conditional.2
  1137.9 58.3 %all_to_all.33 = f32[4,64,512]{2,1,0:T(8,128)S(1)} all-to-all(f32[4,64,512]{2,1,0:T(8,128)S(1)} %bitcast.72), channel_id=1, replica_groups=mesh['width'=4,'row'=4,'src'=2] {'row'}, dimensions={0} | all-to-all | bytes 1048576 | tf_op jit(solution)/shard_map/all_to_all | solution.py:119
  1201.1 8.4 all-to-all-done.4
  1212.4 21.0 %reduce-scatter.2.cloned.1.call-done = f32[256,128]{1,0:T(8,128)} async-done(((f32[256,512]{1,0:T(8,128)}), f32[256,128]{1,0:T(8,128)}) %reduce-scatter.2.cloned.1.call-update) | async-done | bytes 131088 | tf_op jit(solution)/shard_map/reduce_scatter | solution.py:131
  1234.5 18.5 %psum.7 = f32[256]{0:T(256)S(1)} all-reduce(f32[256]{0:T(256)S(1)} %reduce_sum.30), channel_id=1, replica_groups=mesh['width'=4,'row'=4,'src'=2] {'width','src'}, use_global_device_ids=true, to_apply=%region_11.12 | all-reduce | flops 256 | bytes 2048 | tf_op jit(solution)/shard_map/psum | solution.py:132
  (365 shorter events, 545.8 us)
Async XLA Ops:
  8.3 10.1 all-to-all-start.1
  18.4 17.9 %all-to-all-start.2 = ((bf16[4,64,2048]{2,1,0:T(8,128)(2,1)}), bf16[4,64,2048]{2,1,0:T(8,128)(2,1)S(1)}, u32[]{:S(2)}, u32[]{:S(2)}) async-start(bf16[4,64,2048]{2,1,0:T(8,128)(2,1)} %fusion.8), calls=%async_computation.2 | async-start | bytes 2097152 | tf_op jit(solution)/shard_map/all_to_all | solution.py:47
  21.9 331.6 %all-gather.5.cloned.1.call-start = ((), (), s32[]{:S(2)}) async-start(), calls=%async_computation.7 | async-start | bytes 20971520 | tf_op jit(solution)/shard_map/all_gather | solution.py:74
  22.1 0.5 copy-start.3
  22.2 0.6 copy-start.2
  38.1 3.2 copy-start
  61.2 6.7 copy-start.1
  67.1 447.3 %all-gather.3.cloned.1.call-start = ((), (), s32[]{:S(2)}) async-start(), calls=%async_computation.6 | async-start | bytes 37748736 | tf_op jit(solution)/shard_map/all_gather | solution.py:78
  69.2 14.8 %all-to-all-start = ((bf16[2,256,1024]{2,1,0:T(8,128)(2,1)}), bf16[2,256,1024]{2,1,0:T(8,128)(2,1)S(1)}, u32[]{:S(2)}, u32[]{:S(2)}) async-start(bf16[2,256,1024]{2,1,0:T(8,128)(2,1)} %fusion.9), calls=%async_computation | async-start | bytes 2097152 | tf_op jit(solution)/shard_map/all_to_all | solution.py:54
  576.7 111.3 %copy-start.4 = (s32[256]{0:T(256)S(1)}, s32[256]{0:T(256)}, u32[]{:S(2)}) copy-start(s32[256]{0:T(256)} %copy-done.3) | copy-start | bytes 3076
  1197.4 12.1 all-to-all-start.4
  1201.1 32.3 %reduce-scatter.2.cloned.1.call-start = ((), (), s32[]{:S(2)}) async-start(), calls=%async_computation.8 | async-start | bytes 655360 | tf_op jit(solution)/shard_map/reduce_scatter | solution.py:131
Sparse Core Ops, SparseCore 0:
  67.2 286.3 all-gather.4
  355.4 158.8 all-gather.2
  1212.5 20.8 reduce-scatter.1
where the time goes:
time: 1270 us; the launch traced here: 1260 us
  waiting for transfers between devices  426 us (34%)
  matrix products  250 us (20%)
  local copies, waits for them, and re-layouts  241 us (19%)
  other arithmetic  151 us (12%)
  blocking collectives  85.6 us (7%)
  loops' own time  79.6 us (6%)
  starting transfers between devices  15.3 us (1%)
  between operations  13.3 us (1%)
    all_gather x1, waiting for transfers between devices, body(): weights = lax.all_gather(weights, 'width', axis=0, tiled=True)  264 us
    dot_general x30, matrix products, compute(): jnp.einsum('hij,jhe->ije', attend, source_images, preferred_element_type=...  180 us
    while x3, local copies, waits for them, and re-layouts, body(): lax.fori_loop(0, turns, tile, jnp.zeros((row_count, col_count), jnp.float...  168 us
    all_gather x1, waiting for transfers between devices, body(): portion = lax.all_gather(proj_heads, ('row', 'src'), axis=0, tiled=True)  104 us
    reduce_min x64, other arithmetic, tile(): jnp.min(col_slice)  90.4 us
    another operation x1, loops' own time, body(): lax.fori_loop(0, turns, tile, jnp.zeros((row_count, col_count), jnp.float...  78.1 us
    dot_general x1, matrix products, body(): jnp.einsum('jhd,hde->jhe', chosen, portion, preferred_element_type=jnp.fl...  62.4 us
    all_to_all x1, blocking collectives, body(): lax.all_to_all(partial_value, 'row', split_axis=0, concat_axis=0, tiled=T...  58.3 us
  transfers between devices with their start and end apart: 7, of which 7 were waited for; matrix products, arithmetic and copies ran while one was open for 5% of the time, Pallas kernels for 0%

commit v1 on v0

--- a/solution.py
+++ b/solution.py
@@ -7,6 +7,16 @@
 H = 64
 KV = 8
 HD = 128
+
+
+def gather_by_hops(value, name, along):
+    peers = lax.axis_size(name)
+    block, blocks = (value, [value])
+    for _ in range(peers - 1):
+        block = lax.ppermute(block, name, [(i, (i + 1) % peers) for i in range(peers)])
+        blocks.insert(0, block)
+    merged = jnp.concatenate(blocks, axis=along)
+    return jnp.roll(merged, (lax.axis_index(name) + 1) * value.shape[along], axis=along)
 
 
 def combined_all(shard, axis, combine):
@@ -71,7 +81,7 @@
     weights = jnp.where(
         causal, jnp.exp(masked - row_peak[..., None]) / row_mass[..., None], 0.0
     ).astype(jnp.bfloat16)
-    weights = lax.all_gather(weights, "width", axis=0, tiled=True)
+    weights = gather_by_hops(weights, "width", 0)
     value_heads = value_rows.reshape(col_count, KV, HD)
     out_cols = out_proj.shape[1]
     proj_heads = out_proj.reshape(-1, HD, out_cols)

time: 1270 us -> 1210 us (0.953)
  waiting for transfers between devices: 426 us -> 317 us
  local copies, waits for them, and re-layouts: 241 us -> 279 us
    all_gather x1 -> x0, waiting for transfers between devices: 264 us -> none  [body(): weights = lax.all_gather(weights, 'width', axis=0, tiled=True)]
    ppermute x0 -> x3, waiting for transfers between devices: none -> 252 us  [gather_by_hops(): lax.ppermute(block, name, [(i, (i + 1) % peers) for i in range(peers)])]
    all_gather x1, waiting for transfers between devices: 104 us -> 0.01 us  [body(): portion = lax.all_gather(proj_heads, ('row', 'src'), axis=0, tiled=True)]
    unnamed x14 -> x28, local copies, waits for them, and re-layouts: 4.98 us -> 28.4 us
    dynamic_slice x0 -> x1, local copies, waits for them, and re-layouts: none -> 13.8 us  [gather_by_hops(): jnp.roll(merged, (lax.axis_index(name) + 1) * value.shape[along], axis=al...]
  transfers between devices with their start and end apart: 7 -> 9, of which waited for: 7 -> 8; matrix products, arithmetic and copies ran while one was open for 5% -> 11% of each run, Pallas kernels for 0% -> 0%
where the time goes in v1:
time: 1210 us; the launch traced here: 1200 us
  waiting for transfers between devices  317 us (26%)
  local copies, waits for them, and re-layouts  279 us (23%)
  matrix products  253 us (21%)
  other arithmetic  158 us (13%)
  blocking collectives  87.4 us (7%)
  loops' own time  78.7 us (7%)
  starting transfers between devices  16.9 us (1%)
  between operations  13.7 us (1%)
    ppermute x3, waiting for transfers between devices, gather_by_hops(): lax.ppermute(block, name, [(i, (i + 1) % peers) for i in range(peers)])  252 us
    dot_general x30, matrix products, compute(): jnp.einsum('hij,jhe->ije', attend, source_images, preferred_element_type=...  180 us
    while x3, local copies, waits for them, and re-layouts, body(): lax.fori_loop(0, turns, tile, jnp.zeros((row_count, col_count), jnp.float...  168 us
    reduce_min x64, other arithmetic, tile(): jnp.min(col_slice)  90.8 us
    another operation x1, loops' own time, body(): lax.fori_loop(0, turns, tile, jnp.zeros((row_count, col_count), jnp.float...  77.3 us
    dot_general x1, matrix products, body(): jnp.einsum('jhd,hde->jhe', chosen, portion, preferred_element_type=jnp.fl...  62.3 us
    all_to_all x1, blocking collectives, body(): lax.all_to_all(partial_value, 'row', split_axis=0, concat_axis=0, tiled=T...  59.9 us
    dynamic_update_slice x64, local copies, waits for them, and re-layouts, tile(): return lax.dynamic_update_slice(running, result, (row_start, col_start))  56.5 us
  transfers between devices with their start and end apart: 9, of which 8 were waited for; matrix products, arithmetic and copies ran while one was open for 11% of the time, Pallas kernels for 0%

profile of v1, /device:TPU:0, one launch (start us, length us, event | category | flops | bytes accessed | tf_op | source)
XLA Modules:
  0.0 1203.6 jit_solution(3150298542242354196)
XLA Ops:
  24.0 24.2 %all-to-all-done.2 = bf16[4,64,2048]{2,1,0:T(8,128)(2,1)S(1)} async-done(((bf16[4,64,2048]{2,1,0:T(8,128)(2,1)}), bf16[4,64,2048]{2,1,0:T(8,128)(2,1)S(1)}, u32[]{:S(2)}, u32[]{:S(2)}) %all-to-all-start.2) | async-done | bytes 1048608 | tf_op jit(solution)/shard_map/all_to_all | solution.py:57
  53.2 9.3 copy.29
  80.9 90.8 %collective-permute-done = bf16[16,256,512]{2,1,0:T(8,128)(2,1)S(1)} collective-permute-done((bf16[16,256,512]{2,1,0:T(8,128)(2,1)S(1)}, bf16[16,256,512]{2,1,0:T(8,128)(2,1)S(1)}, u32[]{:S(2)}, u32[]{:S(2)}) %collective-permute-start) | collective-permute-done | bytes 4194336 | tf_op jit(solution)/shard_map/ppermute | solution.py:16
  173.7 91.7 %collective-permute-done.1 = bf16[16,256,512]{2,1,0:T(8,128)(2,1)} collective-permute-done((bf16[16,256,512]{2,1,0:T(8,128)(2,1)S(1)}, bf16[16,256,512]{2,1,0:T(8,128)(2,1)}, u32[]{:S(2)}, u32[]{:S(2)}) %collective-permute-start.1) | collective-permute-done | bytes 4194336 | tf_op jit(solution)/shard_map/ppermute | solution.py:16
  270.3 10.4 all-to-all-done
  286.6 69.7 %collective-permute-done.2 = bf16[16,256,512]{2,1,0:T(8,128)(2,1)} collective-permute-done((bf16[16,256,512]{2,1,0:T(8,128)(2,1)}, bf16[16,256,512]{2,1,0:T(8,128)(2,1)}, u32[]{:S(2)}, u32[]{:S(2)}) %collective-permute-start.2) | collective-permute-done | bytes 4194336 | tf_op jit(solution)/shard_map/ppermute | solution.py:16
  388.2 13.8 %constant_dynamic-slice_fusion = bf16[64,256,512]{2,1,0:T(8,128)(2,1)} fusion(bf16[128,256,512]{2,1,0:T(8,128)(2,1)} %constant_dynamic-update-slice_fusion, s32[]{:T(128)S(6)} %select_n.184), kind=kLoop, calls=%fused_computation.52 | loop fusion | bytes 33554436 | tf_op jit(solution)/shard_map/jit(_roll_dynamic)/dynamic_slice | solution.py:19
  402.0 56.4 %copy.31 = bf16[64,256,512]{0,1,2:T(8,128)(2,1)} copy(bf16[64,256,512]{2,1,0:T(8,128)(2,1)} %constant_dynamic-slice_fusion) | data formatting | bytes 33554432 | tf_op jit(solution)/shard_map/while | solution.py:127
  458.4 62.3 %convert_bitcast_fusion = bf16[512,64,2048]{2,0,1:T(8,128)(2,1)} fusion(bf16[64,128,2048]{2,1,0:T(8,128)(2,1)} %all-gather.2.cloned.1.call-done, bf16[512,64,128]{2,1,0:T(8,128)(2,1)} %convert_bitcast_fusion.1), kind=kOutput, calls=%fused_computation.7 | convolution fusion | flops 17246978048 | bytes 176160768 | tf_op jit(solution)/shard_map/jhd,hde->jhe/dot_general | solution.py:97
  520.7 111.3 %copy.30 = bf16[512,64,2048]{2,1,0:T(8,128)(2,1)} copy(bf16[512,64,2048]{2,0,1:T(8,128)(2,1)} %convert_bitcast_fusion) | data formatting | bytes 268435456 | tf_op jit(solution)/shard_map/while | solution.py:127
  632.1 449.3 %while.10 = (s32[]{:T(128)}, f32[256,512]{0,1:T(8,128)S(1)}, s32[256]{0:T(256)S(1)}, s32[512]{0:T(512)}, bf16[512,64,2048]{2,1,0:T(8,128)(2,1)}, /*index=5*/bf16...) while((s32[]{:T(128)}, f32[256,512]{0,1:T(8,128)S(1)}, ...), condition=%wide.region_8.9_spmd, body=%wide.region_2.8_spmd.sunk | while | flops 545257600 | bytes 8939898 | solution.py:127
  645.5 6.0 conditional.2
  714.1 6.0 conditional.2
  724.5 6.0 conditional.2
  735.0 6.0 conditional.2
  745.5 6.0 conditional.2
  756.0 6.0 conditional.2
  766.4 6.0 conditional.2
  776.9 6.0 conditional.2
  787.4 6.0 conditional.2
  1081.5 59.9 %all_to_all.33 = f32[4,64,512]{2,1,0:T(8,128)S(1)} all-to-all(f32[4,64,512]{2,1,0:T(8,128)S(1)} %bitcast.74), channel_id=1, replica_groups=mesh['width'=4,'row'=4,'src'=2] {'row'}, dimensions={0} | all-to-all | bytes 1048576 | tf_op jit(solution)/shard_map/all_to_all | solution.py:129
  1146.2 7.8 all-to-all-done.4
  1156.9 18.6 %reduce-scatter.2.cloned.1.call-done = f32[256,128]{1,0:T(8,128)} async-done(((f32[256,512]{1,0:T(8,128)}), f32[256,128]{1,0:T(8,128)}) %reduce-scatter.2.cloned.1.call-update) | async-done | bytes 131088 | tf_op jit(solution)/shard_map/reduce_scatter | solution.py:141
  1176.5 18.6 %psum.7 = f32[256]{0:T(256)S(1)} all-reduce(f32[256]{0:T(256)S(1)} %reduce_sum.30), channel_id=1, replica_groups=mesh['width'=4,'row'=4,'src'=2] {'width','src'}, use_global_device_ids=true, to_apply=%region_11.12 | all-reduce | flops 256 | bytes 2048 | tf_op jit(solution)/shard_map/psum | solution.py:142
  (386 shorter events, 593.8 us)
Async XLA Ops:
  6.5 451.9 %all-gather.2.cloned.1.call-start = ((), (), s32[]{:S(2)}) async-start(), calls=%async_computation.6 | async-start | bytes 37748736 | tf_op jit(solution)/shard_map/all_gather | solution.py:88
  9.0 10.1 all-to-all-start.1
  19.1 29.0 %all-to-all-start.2 = ((bf16[4,64,2048]{2,1,0:T(8,128)(2,1)}), bf16[4,64,2048]{2,1,0:T(8,128)(2,1)S(1)}, u32[]{:S(2)}, u32[]{:S(2)}) async-start(bf16[4,64,2048]{2,1,0:T(8,128)(2,1)} %fusion.8), calls=%async_computation.2 | async-start | bytes 2097152 | tf_op jit(solution)/shard_map/all_to_all | solution.py:57
  22.9 0.5 copy-start.5
  23.0 0.6 copy-start.4
  62.5 14.2 %copy-start = (f32[16,256,512]{2,1,0:T(8,128)S(1)}, f32[16,256,512]{2,1,0:T(8,128)}, u32[]{:S(2)}) copy-start(f32[16,256,512]{2,1,0:T(8,128)} %copy.29) | copy-start | bytes 25165828
  67.7 197.7 %copy-start.3 = (bf16[512,1024]{1,0:T(8,128)(2,1)S(1)}, bf16[512,1024]{1,0:T(8,128)(2,1)}, u32[]{:S(2)}) copy-start(bf16[512,1024]{1,0:T(8,128)(2,1)} %param.10) | copy-start | bytes 3145732
  78.9 92.8 %collective-permute-start = (bf16[16,256,512]{2,1,0:T(8,128)(2,1)S(1)}, bf16[16,256,512]{2,1,0:T(8,128)(2,1)S(1)}, u32[]{:S(2)}, u32[]{:S(2)}) collective-permute-start(bf16[16,256,512]{2,1,0:T(8,128)(2,1)S(1)} %select_convert_fusion), channel_id=1, source_target_pairs={{0,8},{8,16},{16,24},{24,0},{1,9},{9,17},{17,25},{25,1},{2,10},{10... | collective-permute-start | bytes 12582920 | tf_op jit(solution)/shard_map/ppermute | solution.py:16
  171.7 2.0 copy-start.1
  173.7 91.7 %collective-permute-start.1 = (bf16[16,256,512]{2,1,0:T(8,128)(2,1)S(1)}, bf16[16,256,512]{2,1,0:T(8,128)(2,1)}, u32[]{:S(2)}, u32[]{:S(2)}) collective-permute-start(bf16[16,256,512]{2,1,0:T(8,128)(2,1)S(1)} %collective-permute-done), channel_id=1, source_target_pairs={{0,8},{8,16},{16,24},{24,0},{1,9},{9,17},{17,25},{25,1},{2,10},{10... | collective-permute-start | bytes 12582920 | tf_op jit(solution)/shard_map/ppermute | solution.py:16
  265.4 91.0 %collective-permute-start.2 = (bf16[16,256,512]{2,1,0:T(8,128)(2,1)}, bf16[16,256,512]{2,1,0:T(8,128)(2,1)}, u32[]{:S(2)}, u32[]{:S(2)}) collective-permute-start(bf16[16,256,512]{2,1,0:T(8,128)(2,1)} %collective-permute-done.1), channel_id=1, source_target_pairs={{0,8},{8,16},{16,24},{24,0},{1,9},{9,17},{17,25},{25,1},{2,10},{10... | collective-permute-start | bytes 12582920 | tf_op jit(solution)/shard_map/ppermute | solution.py:16
  266.7 14.0 %all-to-all-start = ((bf16[2,256,1024]{2,1,0:T(8,128)(2,1)}), bf16[2,256,1024]{2,1,0:T(8,128)(2,1)S(1)}, u32[]{:S(2)}, u32[]{:S(2)}) async-start(bf16[2,256,1024]{2,1,0:T(8,128)(2,1)} %fusion.9), calls=%async_computation | async-start | bytes 2097152 | tf_op jit(solution)/shard_map/all_to_all | solution.py:64
  286.6 79.0 %copy-start.2 = (bf16[16,256,512]{2,1,0:T(8,128)(2,1)S(1)}, bf16[16,256,512]{2,1,0:T(8,128)(2,1)}, u32[]{:S(2)}) copy-start(bf16[16,256,512]{2,1,0:T(8,128)(2,1)} %copy-done.1) | copy-start | bytes 12582916
  361.0 7.2 slice-start
  365.7 3.7 slice-start.1
  520.7 111.3 %copy-start.6 = (s32[256]{0:T(256)S(1)}, s32[256]{0:T(256)}, u32[]{:S(2)}) copy-start(s32[256]{0:T(256)} %copy-done.5) | copy-start | bytes 3076
  1142.6 11.4 all-to-all-start.4
  1146.1 29.4 %reduce-scatter.2.cloned.1.call-start = ((), (), s32[]{:S(2)}) async-start(), calls=%async_computation.7 | async-start | bytes 655360 | tf_op jit(solution)/shard_map/reduce_scatter | solution.py:141
Sparse Core Ops, SparseCore 0:
  9.2 173.5 all-gather.1
  1157.0 18.4 reduce-scatter.1
